TPU v7x, 256 devices: a whole 4x4x8 slice. The times are simulated.
256 devices in a mesh: leaf: 8 (over x, core), rows: 32 (over z, y).
Axes of the slice: x: 4, y: 4, z: 8, core: 2. Of those that a mesh axis runs over, the one named last changes fastest.
Arguments:
- leaf_inverse: bfloat16 [16384, 2048], P(('leaf', 'rows')), may hold values from -0.125 to 0.125
- leaf_panel: bfloat16 [245760, 2048], P(('leaf', 'rows')), may hold values from -0.0625 to 0.0625
- mid_inverse: bfloat16 [8192, 2048], P(('leaf', 'rows')), may hold values from -0.125 to 0.125
- mid_panel: bfloat16 [122880, 2048], P(('leaf', 'rows')), may hold values from -0.0625 to 0.0625
- top_inverse: bfloat16 [4096, 2048], P(('leaf', 'rows')), may hold values from -0.125 to 0.125
- top_panel: bfloat16 [61440, 2048], P(('leaf', 'rows')), may hold values from -0.0625 to 0.0625
- leaf_rhs: bfloat16 [128, 16384], P(None, ('leaf', 'rows')), may hold values from -6 to 6
- mid_rhs: bfloat16 [128, 8192], P(None, ('leaf', 'rows')), may hold values from -6 to 6
- top_rhs: bfloat16 [128, 4096], P(None, ('leaf', 'rows')), may hold values from -6 to 6
- outer_solution: bfloat16 [128, 61440], P(None, ('leaf', 'rows')), may hold values from -6 to 6
- leaf_targets: int32 [8, 240], replicated, may hold values from -1 to 255, as said below
- mid_targets: int32 [4, 240], replicated, may hold values from -1 to 255, as said below
- front_counts: int32 [14, 2], replicated, may hold values from 128 to 30720, as said below
Outputs:
- leaf_solution: bfloat16 [128, 16384], P(None, ('leaf', 'rows'))
- mid_solution: bfloat16 [128, 8192], P(None, ('leaf', 'rows'))
- top_solution: bfloat16 [128, 4096], P(None, ('leaf', 'rows'))
- top_contribution: bfloat16 [128, 61440], P(None, ('leaf', 'rows'))
Inputs may be any that keep to these rules, and one draw needn't show every extreme that they name: `front_counts`: row f gives a front's live pivot count and live update row count, leaf fronts first, then middle, then top fronts. Both are positive multiples of 128, at most 2048 and 30720; top front 0 has 2048 pivots and 30720 update rows. A child's update blocks never outnumber its parent's live blocks. `leaf_targets`: row c lists, for each update block j of leaf front c below its live update rows / 128, the block of middle front c // 2 that receives it, and -1 for the other j. The listed blocks are strictly increasing and live in the parent: below its pivot count / 128, or from 16 up to that plus its update rows / 128. `mid_targets`: row c lists, for each update block j of middle front c below its live update rows / 128, the block of top front c // 2 that receives it, and -1 for the other j. The listed blocks are strictly increasing and live in the parent, as for leaf_targets.
All inputs are finite; a program needn't handle non-finite values.
Results may differ from a plain program's by a relative error of at most 0.019.
Values may be sent and summed in bfloat16 or wider, within the bound.
A program may use at most 64 MiB of HBM per device.

v0:
```python
import jax
import jax.numpy as jnp
from jax import lax
from jax.sharding import PartitionSpec as P

FRONT_ROWS = 32768
PIVOTS = 2048
UPDATES = 30720


def from_partner(value, axis, stride):
    mask = 2**stride
    pairs = [(source, source ^ mask) for source in range(lax.axis_size(axis))]
    return lax.ppermute(value, axis, pairs)


def share_sections(piece_part, height, within):
    if height == 0:
        return piece_part
    current = piece_part
    for bit_index in range(height):
        partner = from_partner(current, "leaf", bit_index)
        upper_bit = within // (1 << bit_index) % 2
        lower_first = jnp.concatenate([current, partner], axis=1)
        upper_first = jnp.concatenate([partner, current], axis=1)
        current = jnp.where(upper_bit == 0, lower_first, upper_first)
    return current


def total_sections(partials, height, within):
    if height == 0:
        return partials[:, 0]
    current = partials
    for bit_index in reversed(range(height)):
        halves = current.reshape(current.shape[0], 2, current.shape[1] // 2, current.shape[2])
        upper_bit = within // (1 << bit_index) % 2
        keeping = lax.dynamic_index_in_dim(halves, upper_bit, 1, keepdims=False)
        sending = lax.dynamic_index_in_dim(halves, 1 - upper_bit, 1, keepdims=False)
        current = keeping + from_partner(sending.astype(jnp.bfloat16), "leaf", bit_index).astype(
            sending.dtype
        )
    return current[:, 0]


def place_level(height, section, row_index, row_count):
    group_width = 1 << height
    within = section % group_width
    front_index = section // group_width
    member = within * row_count + row_index
    return (group_width, within, front_index, member)


def live_rows(member, length, count):
    return (member * length + jnp.arange(length) < count)[None, :]


def block_onehot(targets, front_index, start_block, slab_blocks):
    target_row = lax.dynamic_index_in_dim(targets, front_index, 0, keepdims=False)
    target_row = lax.dynamic_slice_in_dim(target_row, start_block, slab_blocks)
    return (target_row[:, None] == jnp.arange(FRONT_ROWS // 128)[None, :]).astype(jnp.bfloat16)


def extend_children(update, height, targets, section, row_index, row_count):
    group_width, within, front_index, member = place_level(height, section, row_index, row_count)
    slab = lax.all_to_all(update, "rows", split_axis=0, concat_axis=1, tiled=True)
    narrow = slab.shape[0]
    slab_blocks = slab.shape[1] // 128
    onehot = block_onehot(targets, front_index, within * slab_blocks, slab_blocks)
    spread = jnp.einsum(
        "cjr,jb->cbr",
        slab.reshape(narrow, slab_blocks, 128),
        onehot,
        preferred_element_type=jnp.float32,
    )
    parent_width = 2 * group_width
    flattened = spread.reshape(narrow, FRONT_ROWS)
    pivot_side = flattened[:, :PIVOTS].reshape(narrow, parent_width, row_count, -1)
    update_side = flattened[:, PIVOTS:].reshape(narrow, parent_width, row_count, -1)
    joined = jnp.concatenate([pivot_side, update_side], axis=3).reshape(narrow, parent_width, -1)
    returned = lax.all_to_all(
        joined.astype(jnp.bfloat16), "rows", split_axis=2, concat_axis=0, tiled=True
    ).astype(joined.dtype)
    return total_sections(returned, height + 1, section % parent_width)


def descend_children(full_local, height, targets, section, row_count, pivot_local):
    group_width = 1 << height
    within = section % group_width
    columns_form = lax.all_to_all(full_local, "rows", split_axis=0, concat_axis=1, tiled=True)
    narrow = columns_form.shape[0]
    shared = share_sections(columns_form[:, None, :], height, within)
    parted = shared.reshape(narrow, group_width, row_count, -1)
    parent_full = jnp.concatenate(
        [
            parted[..., :pivot_local].reshape(narrow, PIVOTS),
            parted[..., pivot_local:].reshape(narrow, UPDATES),
        ],
        axis=1,
    )
    child_width = group_width // 2
    child_within = section % child_width
    child_front = section // child_width
    slab_blocks = UPDATES // (child_width * 128)
    onehot = block_onehot(targets, child_front, child_within * slab_blocks, slab_blocks)
    picked = jnp.einsum(
        "cbr,jb->cjr",
        parent_full.reshape(narrow, FRONT_ROWS // 128, 128),
        onehot,
        preferred_element_type=jnp.float32,
    )
    picked = picked.reshape(narrow, slab_blocks * 128).astype(jnp.bfloat16)
    return lax.all_to_all(picked, "rows", split_axis=1, concat_axis=0, tiled=True)


def separate_sums(partials, group_width, height, within):
    shaped = partials.reshape(partials.shape[0], group_width, -1)
    summed = lax.psum_scatter(
        shaped.astype(jnp.bfloat16), "rows", scatter_dimension=2, tiled=True
    ).astype(jnp.float32)
    return total_sections(summed, height, within)


def body(
    leaf_inverse,
    leaf_panel,
    mid_inverse,
    mid_panel,
    top_inverse,
    top_panel,
    leaf_rhs,
    mid_rhs,
    top_rhs,
    outer_solution,
    leaf_targets,
    mid_targets,
    front_counts,
):
    row_count = lax.axis_size("rows")
    leaf_count = lax.axis_size("leaf")
    section = lax.axis_index("leaf")
    row_index = lax.axis_index("rows")
    inverses = (leaf_inverse, mid_inverse, top_inverse)
    panels = (leaf_panel, mid_panel, top_panel)
    sources = (leaf_rhs, mid_rhs, top_rhs)
    targets = (leaf_targets, mid_targets)
    offsets = (0, leaf_count, leaf_count + leaf_count // 2)
    carried = None
    forward = []
    top_contribution = None
    for height in range(3):
        group_width, within, front_index, member = place_level(
            height, section, row_index, row_count
        )
        inverse = inverses[height]
        panel_rows = panels[height]
        pivot_local = inverse.shape[0]
        pivot_live = live_rows(member, pivot_local, front_counts[offsets[height] + front_index, 0])
        update_live = live_rows(
            member, panel_rows.shape[0], front_counts[offsets[height] + front_index, 1]
        )
        source = sources[height].astype(jnp.float32)
        if carried is not None:
            source = source + carried[:, :pivot_local]
        assembled_local = jnp.where(pivot_live, source, 0.0).astype(jnp.bfloat16)
        gathered = lax.all_gather(assembled_local, "rows", axis=1, tiled=True)
        assembled = share_sections(gathered[:, None, :], height, within).reshape(
            gathered.shape[0], PIVOTS
        )
        solved = jnp.einsum("cp,rp->cr", assembled, inverse, preferred_element_type=jnp.float32)
        solved = jnp.where(pivot_live, solved, 0.0).astype(jnp.bfloat16)
        update = -jnp.einsum("cp,rp->cr", assembled, panel_rows, preferred_element_type=jnp.float32)
        if carried is not None:
            update = carried[:, pivot_local:] + update
        update = jnp.where(update_live, update, 0.0).astype(jnp.bfloat16)
        forward.append(solved)
        if height < 2:
            carried = extend_children(
                update, height, targets[height], section, row_index, row_count
            )
        else:
            top_contribution = update
    solutions = [None, None, None]
    given_rows = outer_solution
    for height in (2, 1, 0):
        group_width, within, front_index, member = place_level(
            height, section, row_index, row_count
        )
        inverse = inverses[height]
        panel_rows = panels[height]
        pivot_local = inverse.shape[0]
        pivot_live = live_rows(member, pivot_local, front_counts[offsets[height] + front_index, 0])
        update_live = live_rows(
            member, panel_rows.shape[0], front_counts[offsets[height] + front_index, 1]
        )
        given_rows = jnp.where(update_live, given_rows, jnp.zeros_like(given_rows))
        partials = jnp.dot(forward[height], inverse, preferred_element_type=jnp.float32) - jnp.dot(
            given_rows, panel_rows, preferred_element_type=jnp.float32
        )
        if height == 0:
            solution = separate_sums(partials, group_width, height, within)
        else:
            solution = separate_sums(partials, group_width, height, within)
        solution = jnp.where(pivot_live, solution, 0.0).astype(jnp.bfloat16)
        solutions[height] = solution
        if height > 0:
            full_local = jnp.concatenate([solution, given_rows], axis=1)
            given_rows = descend_children(
                full_local, height, targets[height - 1], section, row_count, pivot_local
            )
    return (solutions[0], solutions[1], solutions[2], top_contribution)


def solution(mesh):
    placed = (
        P(("leaf", "rows"), None),
        P(("leaf", "rows"), None),
        P(("leaf", "rows"), None),
        P(("leaf", "rows"), None),
        P(("leaf", "rows"), None),
        P(("leaf", "rows"), None),
        P(None, ("leaf", "rows")),
        P(None, ("leaf", "rows")),
        P(None, ("leaf", "rows")),
        P(None, ("leaf", "rows")),
        P(),
        P(),
        P(),
    )
    return jax.shard_map(
        body,
        mesh=mesh,
        in_specs=placed,
        out_specs=(
            P(None, ("leaf", "rows")),
            P(None, ("leaf", "rows")),
            P(None, ("leaf", "rows")),
            P(None, ("leaf", "rows")),
        ),
        check_vma=False,
    )
```

profile of v0, /device:TPU:1, one launch (start us, length us, event | category | flops | bytes accessed | tf_op | source)
XLA Modules:
  0.0 1116.3 jit_solution(15445964068958309150)
XLA Ops:
  10.7 42.3 %all_gather.9 = bf16[128,2048]{0,1:T(8,128)(2,1)S(1)} all-gather(bf16[128,64]{0,1:T(8,128)(2,1)S(1)} %select_convert_fusion.1), channel_id=1, replica_groups=mesh['leaf'=8,'rows'=32] {'rows'}, dimensions={1}, use_global_device_ids=true | all-gather | bytes 540672 | tf_op jit(solution)/shard_map/all_gather | solution.py:165
  64.3 9.7 all-to-all-done
  75.7 9.6 copy.158
  85.4 16.8 %reshape.243 = bf16[32,2,2048]{2,1,0:T(2,128)(2,1)} reshape(bf16[16384,2,4]{2,1,0:T(2,128)(2,1)} %bitcast.148) | data formatting | bytes 524288
  106.1 10.5 all-to-all-done.1
  116.6 19.1 %reshape.244 = bf16[16384,2,4]{2,1,0:T(2,128)(2,1)} reshape(bf16[32,2,2048]{2,1,0:T(2,128)(2,1)S(1)} %all-to-all-done.1) | data formatting | bytes 524288
  135.7 16.5 %copy.159 = bf16[4,2,16384]{2,0,1:T(4,128)(2,1)S(1)} copy(bf16[4,2,16384]{0,1,2:T(2,128)(2,1)} %bitcast.149) | data formatting | bytes 524288 | tf_op jit(solution)/shard_map/all_to_all | solution.py:80
  153.2 15.3 %collective-permute-start = (bf16[128,1,512]{0,2,1:T(8,128)(2,1)S(1)}, bf16[128,1,512]{0,2,1:T(8,128)(2,1)S(1)}, u32[]{:S(2)}, u32[]{:S(2)}) collective-permute-start(bf16[128,1,512]{0,2,1:T(8,128)(2,1)S(1)} %copy.200), channel_id=1, source_target_pairs={{0,32},{32,0},{64,96},{96,64},{128,160},{160,128},{192,224},{224,1... | collective-permute-start | bytes 393224 | tf_op jit(solution)/shard_map/ppermute | solution.py:14
  169.6 34.8 %all_gather.10 = bf16[128,1024]{0,1:T(8,128)(2,1)S(1)} all-gather(bf16[128,32]{0,1:T(8,128)(2,1)S(1)} %fusion.42), channel_id=1, replica_groups=mesh['leaf'=8,'rows'=32] {'rows'}, dimensions={1}, use_global_device_ids=true | all-gather | bytes 270336 | tf_op jit(solution)/shard_map/all_gather | solution.py:165
  204.5 13.3 %collective-permute-start.1 = (bf16[128,1,1024]{0,2,1:T(8,128)(2,1)S(1)}, bf16[128,1,1024]{0,2,1:T(8,128)(2,1)S(1)}, u32[]{:S(2)}, u32[]{:S(2)}) collective-permute-start(bf16[128,1,1024]{0,2,1:T(8,128)(2,1)S(1)} %bitcast.170), channel_id=1, source_target_pairs={{0,32},{32,0},{64,96},{96,64},{128,160},{160,128},{192,224},{224,1... | collective-permute-start | bytes 786440 | tf_op jit(solution)/shard_map/ppermute | solution.py:14
  226.2 8.6 all-to-all-done.2
  243.3 16.8 %reshape.245 = bf16[32,2,2048]{2,1,0:T(2,128)(2,1)} reshape(bf16[8192,4,4]{2,1,0:T(4,128)(2,1)} %bitcast.150) | data formatting | bytes 524288
  264.1 10.3 all-to-all-done.3
  274.4 19.1 %reshape.246 = bf16[8192,4,4]{2,1,0:T(4,128)(2,1)} reshape(bf16[32,2,2048]{2,1,0:T(2,128)(2,1)S(1)} %all-to-all-done.3) | data formatting | bytes 524288
  293.5 10.9 copy.167
  316.6 31.3 %all_gather.11 = bf16[128,512]{0,1:T(8,128)(2,1)S(1)} all-gather(bf16[128,16]{0,1:T(8,128)(2,1)S(1)} %fusion.48), channel_id=1, replica_groups=mesh['leaf'=8,'rows'=32] {'rows'}, dimensions={1}, use_global_device_ids=true | all-gather | bytes 135168 | tf_op jit(solution)/shard_map/all_gather | solution.py:165
  347.9 10.2 collective-permute-start.4
  372.3 209.2 %reduce-scatter.4.cloned.1.call-done = bf16[128,4,16]{0,2,1:T(8,128)(2,1)} async-done(((bf16[128,4,512]{0,2,1:T(8,128)(2,1)}), bf16[128,4,16]{0,2,1:T(8,128)(2,1)}) %reduce-scatter.4.cloned.1.call-update) | async-done | bytes 16400 | tf_op jit(solution)/shard_map/reduce_scatter | solution.py:117
  593.9 15.3 %all_to_all.111 = bf16[32,4,256]{2,1,0:T(4,128)(2,1)S(1)} all-to-all(bf16[32,4,256]{2,1,0:T(4,128)(2,1)S(1)} %all_to_all.92), channel_id=1, replica_groups=mesh['leaf'=8,'rows'=32] {'rows'}, dimensions={0} | all-to-all | bytes 131072 | tf_op jit(solution)/shard_map/all_to_all | solution.py:89
  628.0 6.9 all-to-all-done.5
  637.9 207.7 %reduce-scatter.6.cloned.1.call-done = bf16[128,2,32]{0,2,1:T(8,128)(2,1)} async-done(((bf16[128,2,1024]{0,2,1:T(8,128)(2,1)}), bf16[128,2,32]{0,2,1:T(8,128)(2,1)}) %reduce-scatter.6.cloned.1.call-update) | async-done | bytes 16400 | tf_op jit(solution)/shard_map/reduce_scatter | solution.py:117
  854.0 15.7 %all_to_all.112 = bf16[32,4,512]{2,1,0:T(4,128)(2,1)S(1)} all-to-all(bf16[32,4,512]{2,1,0:T(4,128)(2,1)S(1)} %pad_maximum_fusion.2), channel_id=1, replica_groups=mesh['leaf'=8,'rows'=32] {'rows'}, dimensions={0} | all-to-all | bytes 262144 | tf_op jit(solution)/shard_map/all_to_all | solution.py:89
  882.0 9.8 all-to-all-done.7
  902.6 205.6 %reduce-scatter.8.cloned.1.call-done = bf16[128,1,64]{0,2,1:T(8,128)(2,1)} async-done(((bf16[128,1,2048]{0,2,1:T(8,128)(2,1)}), bf16[128,1,64]{0,2,1:T(8,128)(2,1)}) %reduce-scatter.8.cloned.1.call-update) | async-done | bytes 16400 | tf_op jit(solution)/shard_map/reduce_scatter | solution.py:117
  (179 shorter events, 136.3 us)
Async XLA Ops:
  7.2 211.8 %copy-start = (bf16[480,2048]{1,0:T(8,128)(2,1)S(1)}, bf16[480,2048]{1,0:T(8,128)(2,1)}, u32[]{:S(2)}) copy-start(bf16[480,2048]{1,0:T(8,128)(2,1)} %param.16) | copy-start | bytes 5898244
  58.5 15.4 %all-to-all-start = ((bf16[32,4,960]{2,1,0:T(4,128)(2,1)}), bf16[32,4,960]{2,1,0:T(4,128)(2,1)S(1)}, u32[]{:S(2)}, u32[]{:S(2)}) async-start(bf16[32,4,960]{2,1,0:T(4,128)(2,1)} %all_to_all.84), calls=%async_computation | async-start | bytes 524288 | tf_op jit(solution)/shard_map/all_to_all | solution.py:65
  102.2 14.4 %all-to-all-start.1 = ((bf16[32,2,2048]{2,1,0:T(2,128)(2,1)}), bf16[32,2,2048]{2,1,0:T(2,128)(2,1)S(1)}, u32[]{:S(2)}, u32[]{:S(2)}) async-start(bf16[32,2,2048]{2,1,0:T(2,128)(2,1)} %reshape.243), calls=%async_computation.1 | async-start | bytes 524288 | tf_op jit(solution)/shard_map/all_to_all | solution.py:80
  153.2 16.3 %collective-permute-start = (bf16[128,1,512]{0,2,1:T(8,128)(2,1)S(1)}, bf16[128,1,512]{0,2,1:T(8,128)(2,1)S(1)}, u32[]{:S(2)}, u32[]{:S(2)}) collective-permute-start(bf16[128,1,512]{0,2,1:T(8,128)(2,1)S(1)} %copy.200), channel_id=1, source_target_pairs={{0,32},{32,0},{64,96},{96,64},{128,160},{160,128},{192,224},{224,1... | collective-permute-start | bytes 393224 | tf_op jit(solution)/shard_map/ppermute | solution.py:14
  204.5 14.4 %collective-permute-start.1 = (bf16[128,1,1024]{0,2,1:T(8,128)(2,1)S(1)}, bf16[128,1,1024]{0,2,1:T(8,128)(2,1)S(1)}, u32[]{:S(2)}, u32[]{:S(2)}) collective-permute-start(bf16[128,1,1024]{0,2,1:T(8,128)(2,1)S(1)} %bitcast.170), channel_id=1, source_target_pairs={{0,32},{32,0},{64,96},{96,64},{128,160},{160,128},{192,224},{224,1... | collective-permute-start | bytes 786440 | tf_op jit(solution)/shard_map/ppermute | solution.py:14
  220.5 14.3 %all-to-all-start.2 = ((bf16[32,4,480]{2,1,0:T(4,128)(2,1)}), bf16[32,4,480]{2,1,0:T(4,128)(2,1)S(1)}, u32[]{:S(2)}, u32[]{:S(2)}) async-start(bf16[32,4,480]{2,1,0:T(4,128)(2,1)} %all_to_all.88), calls=%async_computation.2 | async-start | bytes 262144 | tf_op jit(solution)/shard_map/all_to_all | solution.py:65
  260.1 14.3 %all-to-all-start.3 = ((bf16[32,2,2048]{2,1,0:T(2,128)(2,1)}), bf16[32,2,2048]{2,1,0:T(2,128)(2,1)S(1)}, u32[]{:S(2)}, u32[]{:S(2)}) async-start(bf16[32,2,2048]{2,1,0:T(2,128)(2,1)} %reshape.245), calls=%async_computation.3 | async-start | bytes 524288 | tf_op jit(solution)/shard_map/all_to_all | solution.py:80
  264.0 317.5 %reduce-scatter.4.cloned.1.call-start = ((), (), s32[]{:S(2)}) async-start(), calls=%async_computation.11 | async-start | bytes 540672 | tf_op jit(solution)/shard_map/reduce_scatter | solution.py:117
  305.0 62.9 %copy-start.3 = (bf16[16,2048]{1,0:T(8,128)(2,1)S(1)}, bf16[16,2048]{1,0:T(8,128)(2,1)}, u32[]{:S(2)}) copy-start(bf16[16,2048]{1,0:T(8,128)(2,1)} %param.17) | copy-start | bytes 196612
  305.8 4.0 collective-permute-start.2
  309.9 5.9 collective-permute-start.3
  347.9 11.2 %collective-permute-start.4 = (bf16[128,1,512]{0,2,1:T(8,128)(2,1)S(1)}, bf16[128,1,512]{0,2,1:T(8,128)(2,1)S(1)}, u32[]{:S(2)}, u32[]{:S(2)}) collective-permute-start(bf16[128,1,512]{0,2,1:T(8,128)(2,1)S(1)} %bitcast.175), channel_id=1, source_target_pairs={{0,32},{32,0},{64,96},{96,64},{128,160},{160,128},{192,224},{224,1... | collective-permute-start | bytes 393224 | tf_op jit(solution)/shard_map/ppermute | solution.py:14
  359.1 7.7 collective-permute-start.5
  582.2 3.1 collective-permute-start.6
  585.2 7.6 collective-permute-start.7
  609.2 2.7 collective-permute-start.8
  612.0 4.8 collective-permute-start.9
  621.6 13.3 %all-to-all-start.5 = ((bf16[4,32,480]{2,0,1:T(4,128)(2,1)}), bf16[4,32,480]{2,0,1:T(4,128)(2,1)S(1)}, u32[]{:S(2)}, u32[]{:S(2)}) async-start(bf16[4,32,480]{2,0,1:T(4,128)(2,1)} %copy.180), calls=%async_computation.6 | async-start | bytes 262144 | tf_op jit(solution)/shard_map/all_to_all | solution.py:112
  625.4 220.1 %reduce-scatter.6.cloned.1.call-start = ((), (), s32[]{:S(2)}) async-start(), calls=%async_computation.12 | async-start | bytes 540672 | tf_op jit(solution)/shard_map/reduce_scatter | solution.py:117
  637.8 242.4 %copy-start.7 = (pred[64]{0:T(512)(128)(4,1)S(1)}, pred[64]{0:T(512)(128)(4,1)}, u32[]{:S(2)}) copy-start(pred[64]{0:T(512)(128)(4,1)} %copy-done.6) | copy-start | bytes 196
  846.3 6.8 collective-permute-start.10
  869.8 3.2 collective-permute-start.11
  875.4 16.4 %all-to-all-start.7 = ((bf16[4,32,960]{2,0,1:T(4,128)(2,1)}), bf16[4,32,960]{2,0,1:T(4,128)(2,1)}, u32[]{:S(2)}, u32[]{:S(2)}) async-start(bf16[4,32,960]{2,0,1:T(4,128)(2,1)} %copy.187), calls=%async_computation.9 | async-start | bytes 524288 | tf_op jit(solution)/shard_map/all_to_all | solution.py:112
  880.0 228.2 %reduce-scatter.8.cloned.1.call-start = ((), (), s32[]{:S(2)}) async-start(), calls=%async_computation.13 | async-start | bytes 540672 | tf_op jit(solution)/shard_map/reduce_scatter | solution.py:117
  (13 other events, 205.8 us)
Sparse Core Ops, SparseCore 0:
  372.4 208.9 reduce-scatter.3
  638.0 207.5 reduce-scatter.5
  900.4 207.7 reduce-scatter.7
where the time goes:
time: 1130 us; the launch traced here: 1120 us
  waiting for transfers between devices  695 us (62%)
  local copies, waits for them, and re-layouts  139 us (12%)
  blocking collectives  139 us (12%)
  starting transfers between devices  92.1 us (8%)
  matrix products  22.4 us (2%)
  between operations  14.9 us (1%)
  other arithmetic  13.2 us (1%)
    reduce_scatter x3, waiting for transfers between devices, separate_sums(): lax.psum_scatter(shaped.astype(jnp.bfloat16), 'rows', scatter_dimension=2...  622 us
    all_gather x3, blocking collectives, body(): gathered = lax.all_gather(assembled_local, 'rows', axis=1, tiled=True)  108 us
    unnamed x42, local copies, waits for them, and re-layouts  75.2 us
    ppermute x12, starting transfers between devices, from_partner(): return lax.ppermute(value, axis, pairs)  65.7 us
    all_to_all x2, blocking collectives, descend_children(): lax.all_to_all(full_local, 'rows', split_axis=0, concat_axis=1, tiled=True)  31 us
    all_to_all x2, local copies, waits for them, and re-layouts, extend_children(): lax.all_to_all(joined.astype(jnp.bfloat16), 'rows', split_axis=2, concat_...  27.3 us
  transfers between devices with their start and end apart: 21, of which 20 were waited for; matrix products, arithmetic and copies ran while one was open for 1% of the time, Pallas kernels for 0%

commit v1 on v0

v1 whole, which is shorter than its diff:
```python
import jax
import jax.numpy as jnp
from jax import lax
from jax.experimental import pallas as pl
from jax.experimental.pallas import tpu as pltpu
from jax.sharding import PartitionSpec as P

MESH = pl.DeviceIdType.MESH
BF = jnp.bfloat16
F32 = jnp.float32
R = 32

(EA, A1, X1, D1, A2, RT, ZG, P3, U3, D2, CR, HX2, XX2, ZX2, GR1, ZGM, OT, HX1, ZX1, OM, GR0,
 AG0, G1, G2, RS2, RS1, RS0) = tuple(range(21)) + tuple(range(21, 21 + 54, 9))
NSEM = 21 + 54


def pieces(rows, period):
    out = {}
    for d in range(period):
        start = rows * d
        first = start // 128
        last = (start + rows - 1) // 128
        for b in range(first, last + 1):
            out.setdefault(b, []).append((d, b - first))
    return [out[b] for b in range(rows * period // 128)]


MID_PIECES = pieces(480, 4)
TOP_PIECES = pieces(240, 8)


def kernel(
    rhs0, rhs1, rhs2, outer, w0, q0, w1, q1, w2, q2, ltv, mtv, lt, mt, cnt,
    o_leaf, o_mid, o_top, o_con,
    wp0, wp1, wp2, qv0, qv1, qv2, at0, e, at, a, y0, y1, y2, le, sb1, lb1, sp1, rp1, c1, rm, sba1, la1, sb2, lb2, vm,
    s3p, r3p, s3u, r3u, rtq, sba2, la2, gtq, zt, ct, lc, g2, xpt, sbx, rbx, sby, ry, sz, lz, xs2, xx2, gm, zm, lg1,
    g1, sbx1, rbx1, sby1, ry1, sz1, lz1, xsb1, gl, lg0, g0, sbl, ryl, szl, lzl, lot, lom,
    tmp, invv, inv, isem, wsem, ssem, rsem,
):
    s = lax.axis_index("leaf")
    r = lax.axis_index("rows")
    c = s % 2
    w4 = s % 4
    z = r // 4
    y = r % 4
    xb = (s // 2) % 2
    m1 = c * R + r
    m2 = w4 * R + r
    p1 = s + 1 - 2 * c
    p2 = s + 2 - 4 * xb
    p3 = p2 + 1 - 2 * c
    partners = (p1, p2, p3)

    barrier = pltpu.get_barrier_semaphore()

    def greet(k, _):
        pl.semaphore_signal(barrier, inc=1, device_id=(s, (r + k) % R), device_id_type=MESH)
        return 0

    lax.fori_loop(1, R, greet, 0)
    for p in partners:
        pl.semaphore_signal(barrier, inc=1, device_id=(p, r), device_id_type=MESH)

    off0 = pl.multiple_of((r % 2) * 64, 64)
    off1 = pl.multiple_of((r % 4) * 96 % 128, 32)
    off2 = pl.multiple_of((r % 8) * 112 % 128, 16)
    loads = []
    for k, (src, dst) in enumerate((
        (w0, wp0.at[pl.ds(off0, 960)]), (q0, qv0), (w1, wp1.at[pl.ds(off1, 480)]), (q1, qv1),
        (w2, wp2.at[pl.ds(off2, 240)]), (q2, qv2),
    )):
        copy = pltpu.make_async_copy(src, dst, wsem.at[k])
        copy.start()
        loads.append(copy)
    for wp, off, rows in ((wp0, off0, 960), (wp1, off1, 480), (wp2, off2, 240)):
        def zero_pad(t, _, wp=wp, off=off, rows=rows):
            at_row = jnp.where(16 * t < off, 16 * t, 16 * t + rows)
            wp[pl.ds(pl.multiple_of(at_row, 16), 16), :] = jnp.zeros((16, 2048), BF)
            return 0
        lax.fori_loop(0, (wp.shape[0] - rows) // 16, zero_pad, 0)
    zero_block = jnp.zeros((4, 128), BF)
    lb1[0] = zero_block
    vm[0] = zero_block
    vm[121] = zero_block
    ct[60] = zero_block
    zt[0] = zero_block
    zm[0] = zero_block
    gm[120] = zero_block

    piv0, piv1, piv2, upd2 = cnt[0, s], cnt[0, 8 + s // 2], cnt[0, 12 + s // 4], cnt[1, 12 + s // 4]

    def live(pivots, block):
        return jnp.clip(pivots - block * 128, 0, 1).astype(F32)

    f0, f1, f2 = live(piv0, r // 2), live(piv1, m1 // 4), live(piv2, m2 // 8)
    at0[...] = (rhs0[...].astype(F32) * f0).astype(BF)

    place = lax.broadcasted_iota(jnp.int32, (128, 128), 0)
    wanted = lax.broadcasted_iota(jnp.int32, (128, 128), 1)
    for row, (values, here) in enumerate(((ltv, s), (mtv, s // 2))):
        line = values[pl.ds(here, 1), :]
        parts = [line[:, :128], jnp.concatenate([line[:, 128:], jnp.full((1, 16), -1, jnp.int32)], axis=1)]
        found = [jnp.zeros((1, 128), jnp.int32)] * 2
        for k in range(2):
            target = jnp.broadcast_to(parts[k], (128, 128)).T
            j = place + 128 * k
            if row == 0:
                j = 1 + j + j // 15 + (j % 15 > 7).astype(jnp.int32)
            else:
                j = 1 + j
            for h in range(2):
                hit = jnp.where(target == wanted + 128 * h, j, 0)
                found[h] = found[h] + jnp.sum(hit, axis=0, keepdims=True)
        for h in range(2):
            invv[2 * row + h:2 * row + h + 1, :] = found[h]
    table = pltpu.make_async_copy(invv, inv, isem)
    table.start()

    def block_rows(x, rows, first):
        tmp[0:rows] = jnp.zeros((rows, 128), F32)
        tmp[pl.ds(pl.multiple_of(first, 16), x.shape[0]), :] = x
        return [tmp[b * 128:(b + 1) * 128].T for b in range(rows // 128)]

    e[:, 0] = block_rows(rhs1[...].astype(F32) * f1, 128, 32 * (r % 4))[0].reshape(R, 4, 128).astype(BF)
    e[:, 1] = block_rows(rhs2[...].astype(F32) * f2, 128, 16 * (r % 8))[0].reshape(R, 4, 128).astype(BF)
    row240 = lax.broadcasted_iota(jnp.int32, (240, 128), 0)
    given = jnp.where(row240 < upd2 - 240 * m2, outer[...].astype(F32), 0.0)
    for b, v in enumerate(block_rows(given, 384, off2)):
        g2[:, b * 128:(b + 1) * 128] = v.astype(BF)
        e[:, 2 + b] = v.reshape(R, 4, 128).astype(BF)

    pl.semaphore_wait(barrier, R - 1 + 3)

    landed = {}

    def remote(src, dst, n, dev, land):
        landed[n] = [land, False]
        return pltpu.make_async_remote_copy(
            src_ref=src, dst_ref=dst, send_sem=ssem.at[n], recv_sem=rsem.at[n], device_id=dev, device_id_type=MESH
        )

    def to_rows(src_of, dst, n, land):
        def send(k, _):
            d = (r + k) % R
            remote(src_of(d), dst, n, (s, d), land).start()
            return 0

        lax.fori_loop(1, R, send, 0)

    def arrived(n):
        ref = landed[n][0]
        landed[n][1] = True
        pltpu.make_async_copy(ref, ref, rsem.at[n]).wait()

    def sent(n):
        ref = landed[n][0]
        pltpu.make_async_copy(ref, ref, ssem.at[n]).wait()

    def gather(mine, dst, n, piece):
        def along_y(src, k):
            for j in (1, 3, 2):
                remote(src, dst(k), n, (s, z * 4 + (y + j) % 4), piece(24)).start()

        for k in (4, 3, 5, 2, 6, 1, 7):
            remote(mine, dst(r), n + k, (s, (z + k) % 8 * 4 + y), piece(1)).start()
        along_y(mine, r)
        for k in (1, 7, 2, 6, 3, 5, 4):
            arrived(n + k)
            other = (z + 8 - k) % 8 * 4 + y
            along_y(dst(other), other)
        arrived(n)

    def reduce_y(src, land, n, o, piece):
        t = (z + o) % 8
        for j in (1, 3, 2):
            remote(src(4 * t + (y + j) % 4), land.at[o, j - 1], n + o, (s, z * 4 + (y + j) % 4), piece(3)).start()

    def reduce_z(src, land, stage, final, n, o, piece):
        t = (z + o) % 8
        arrived(n + o)
        v = src[4 * t + y].astype(F32) + land[o, 0].astype(F32) + land[o, 1].astype(F32) + land[o, 2].astype(F32)
        if o == 0:
            return v
        stage[o - 1] = v.astype(BF)
        remote(stage.at[o - 1], final.at[o - 1], n + 8, (s, t * 4 + y), piece(7)).start()

    ORDER = (1, 2, 3, 4, 5, 6, 7, 0)

    def nt(x, w):
        return lax.dot_general(x, w, (((1,), (1,)), ((), ())), preferred_element_type=F32)

    at[r] = at0[...]
    gather(at0, lambda k: at.at[k], AG0, lambda k: at.at[pl.ds(0, k)])
    to_rows(lambda d: e.at[d], le.at[r], EA, le.at[pl.ds(0, R - 1)])
    le[r] = e[r]
    for k in range(16):
        block = at[2 * k:2 * k + 2].reshape(128, 128)
        a[:, k * 128:(k + 1) * 128] = block.T
    loads[0].wait()
    loads[1].wait()

    def leaf_update(t, _):
        prod = -nt(a[...], wp0[pl.ds(pl.multiple_of(t * 256, 256), 256), :])
        for b in range(2):
            sb1[:, 2 * t + b] = prod[:, b * 128:(b + 1) * 128].reshape(R, 4, 128).astype(BF)
        return 0

    lax.fori_loop(0, 4, leaf_update, 0)
    to_rows(lambda d: sb1.at[d], lb1.at[pl.ds(1 + r * 8, 8)], A1, lb1.at[pl.ds(0, 8 * (R - 1))])
    lb1[pl.ds(1 + r * 8, 8)] = sb1[r]
    y0[...] = (nt(a[...], qv0[...]) * f0).astype(BF)

    arrived(EA)
    for b in range(8):
        rm[b] = sum(le[4 * b + i, 0].astype(F32) for i in range(4))
    for b in range(4):
        rtq[4 * w4 + b] = sum(le[8 * b + i, 1].astype(F32) for i in range(8)).astype(BF)

    def outer_merge(q, _):
        for i, parts in enumerate(TOP_PIECES):
            v = sum(le[8 * q + d, 2 + k].astype(F32) for d, k in parts).astype(BF)
            gtq[15 * q + i] = v
            zt[17 + 60 * w4 + 15 * q + i] = v
        return 0

    lax.fori_loop(0, 4, outer_merge, 0)
    for p in partners:
        remote(rtq.at[pl.ds(4 * w4, 4)], rtq.at[pl.ds(4 * w4, 4)], RT, (p, r), rtq.at[pl.ds(0, 12)]).start()
        remote(gtq, zt.at[pl.ds(17 + 60 * w4, 60)], ZG, (p, r), zt.at[pl.ds(16, 180)]).start()
    loads[4].wait()
    loads[5].wait()

    def top_given(t, _):
        cols = pl.ds(pl.multiple_of(t * 256, 256), 256)
        xpt[:, cols] = -jnp.dot(g2[...], wp2[:, cols], preferred_element_type=F32)
        return 0

    lax.fori_loop(0, 8, top_given, 0)

    arrived(A1)
    table.wait()

    def leaf_merge(q, _):
        lb1[16 * q + 8] = (lb1[16 * q + 8].astype(F32) + lb1[16 * q + 9].astype(F32)).astype(BF)
        return 0

    lax.fori_loop(0, 16, leaf_merge, 0)

    def child_block(core, j):
        b = jnp.where(j < 8, 8 * core, 8 + 120 * core) + j
        return jnp.clip(inv[b // 128, b % 128], 0, 256)

    def for_partner(j, _):
        sp1[j] = lb1[child_block(1 - c, j)]
        return 0

    lax.fori_loop(0, 128, for_partner, 0, unroll=8)
    remote(sp1, rp1, X1, (p1, r), rp1).start()

    def for_own(j, _):
        c1[j] = lb1[child_block(c, j)].astype(F32)
        return 0

    lax.fori_loop(0, 128, for_own, 0, unroll=8)
    arrived(X1)
    c1[...] = c1[...] + rp1[...].astype(F32)

    sba1[...] = (rm[...] + c1[0:8]).astype(BF)
    la1[c, r] = sba1[...]
    gather(sba1, lambda k: la1.at[c, k], G1, lambda k: la1.at[0, pl.ds(0, k)])
    remote(la1.at[c], la1.at[c], D1, (p1, r), la1.at[1 - c]).start()
    arrived(D1)
    for h in range(2):
        for b in range(8):
            a[:, (8 * h + b) * 128:(8 * h + b + 1) * 128] = la1[h, :, b].reshape(128, 128)
    loads[2].wait()
    loads[3].wait()

    def mid_update(t, _):
        prod = nt(a[...], wp1[pl.ds(pl.multiple_of(t * 128, 128), 128), :])
        sb2[:, t] = prod.reshape(R, 4, 128).astype(BF)
        return 0

    lax.fori_loop(0, 5, mid_update, 0)
    to_rows(lambda d: sb2.at[d], lb2.at[r], A2, lb2.at[pl.ds(0, R - 1)])
    lb2[r] = sb2[r]
    y1[...] = (nt(a[...], qv1[...]) * f1).astype(BF)
    arrived(A2)

    def mid_merge(q, _):
        for i, parts in enumerate(MID_PIECES):
            v = c1[8 + 15 * q + i] - sum(lb2[4 * q + d, k].astype(F32) for d, k in parts)
            vm[1 + 15 * q + i] = v.astype(BF)
        return 0

    lax.fori_loop(0, 8, mid_merge, 0)

    def parent_block(j):
        return jnp.clip(inv[2 + j // 128, j % 128] - 120 * c, 0, 121)

    for j in range(16):
        s3p[j] = vm[parent_block(j)]
    for k, p in enumerate(partners):
        remote(s3p, r3p.at[k], P3, (p, r), r3p).start()
    for k in range(3):
        def top_spread(j, _, k=k):
            s3u[k, j] = vm[parent_block(16 + 60 * (partners[k] % 4) + j)]
            return 0

        lax.fori_loop(0, 60, top_spread, 0, unroll=4)
        remote(s3u.at[k], r3u.at[k], U3, (partners[k], r), r3u).start()
    arrived(RT)
    arrived(P3)
    for j in range(16):
        v = rtq[j].astype(F32) + s3p[j].astype(F32) + sum(r3p[k, j].astype(F32) for k in range(3))
        sba2[j] = v.astype(BF)
    la2[c, r] = sba2[pl.ds(8 * c, 8)]
    gather(sba2.at[pl.ds(8 * c, 8)], lambda k: la2.at[c, k], G2, lambda k: la2.at[0, pl.ds(0, k)])
    arrived(U3)

    def top_sum(j, _):
        v = vm[parent_block(16 + 60 * w4 + j)].astype(F32) + sum(r3u[k, j].astype(F32) for k in range(3))
        ct[j] = v.astype(BF)
        return 0

    lax.fori_loop(0, 60, top_sum, 0, unroll=4)
    remote(la2.at[c], la2.at[c], D2, (p1, r), la2.at[1 - c]).start()
    to_rows(lambda d: ct.at[pl.ds(240 * d // 128, 3)], lc.at[r], CR, lc.at[pl.ds(0, R - 1)])
    lc[r] = ct[pl.ds(240 * r // 128, 3)]
    arrived(D2)
    for h in range(2):
        for b in range(8):
            a[:, (8 * h + b) * 128:(8 * h + b + 1) * 128] = la2[h, :, b].reshape(128, 128)
    y2[...] = (nt(a[...], qv2[...]) * f2).astype(BF)

    def top_partial(t, _):
        cols = pl.ds(pl.multiple_of(t * 256, 256), 256)
        v = xpt[:, cols] + jnp.dot(y2[...], qv2[:, cols], preferred_element_type=F32)
        for b in range(2):
            sbx[t // 4, :, 2 * (t % 4) + b] = v[:, b * 128:(b + 1) * 128].reshape(R, 4, 128).astype(BF)
        return 0

    lax.fori_loop(0, 8, top_partial, 0)
    remote(sbx.at[1 - c], rbx, HX2, (p1, r), rbx).start()
    prod = nt(a[...], wp2[...])
    arrived(CR)
    for b in range(3):
        v = lc[:, b].astype(F32).reshape(128, 128) - prod[:, b * 128:(b + 1) * 128]
        tmp[b * 128:(b + 1) * 128] = v.T
    o_con[...] = jnp.where(row240 < upd2 - 240 * m2, tmp[pl.ds(off2, 240), :], 0.0).astype(BF)
    arrived(HX2)

    def reduce_half(mine, other, both, land, stage, final, n):
        for o in ORDER:
            t = (z + o) % 8
            rows4 = pl.ds(4 * t, 4)
            both[rows4] = (mine[c, rows4].astype(F32) + other[rows4].astype(F32)).astype(BF)
            reduce_y(lambda d: both.at[d], land, n, o, lambda k: land.at[0, pl.ds(0, k)])
        for o in ORDER:
            v = reduce_z(both, land, stage, final, n, o, lambda k: final.at[pl.ds(0, k)])
        arrived(n + 8)
        for o in range(7):
            v = v + final[o].astype(F32)
        return v

    xs2[...] = reduce_half(sbx, rbx, sby, ry, sz, lz, RS2)
    remote(xs2, xx2, XX2, (p2, r), xx2).start()
    arrived(XX2)
    for b in range(8):
        zt[1 + 8 * c + b] = ((xs2[b] + xx2[b]) * live(piv2, 8 * c + b)).astype(BF)
    remote(zt.at[pl.ds(1 + 8 * c, 8)], zt.at[pl.ds(1 + 8 * c, 8)], ZX2, (p1, r), zt.at[pl.ds(0, 8)]).start()
    arrived(ZX2)
    arrived(ZG)

    def mid_pick(j, _):
        v = zt[mt[s // 2, 120 * c + j] + 1]
        gm[j] = v
        zm[17 + 120 * c + j] = v
        return 0

    lax.fori_loop(0, 120, mid_pick, 0, unroll=8)
    to_rows(lambda d: gm.at[pl.ds(480 * d // 128, 5)], lg1.at[r], GR1, lg1.at[pl.ds(0, R - 1)])
    lg1[r] = gm[pl.ds(480 * r // 128, 5)]
    remote(gm.at[pl.ds(0, 120)], zm.at[pl.ds(17 + 120 * c, 120)], ZGM, (p1, r), zm.at[pl.ds(0, 120)]).start()
    to_rows(lambda d: zt.at[1 + 4 * w4 + d // 8], lot.at[r], OT, lot.at[pl.ds(0, R - 1)])
    lot[r] = zt[1 + 4 * w4 + r // 8]
    arrived(GR1)
    for b in range(5):
        g1[:, b * 128:(b + 1) * 128] = lg1[:, b].reshape(128, 128)

    def mid_partial(t, _):
        cols = pl.ds(pl.multiple_of(t * 256, 256), 256)
        v = jnp.dot(y1[...], qv1[:, cols], preferred_element_type=F32) - jnp.dot(
            g1[...], wp1[:, cols], preferred_element_type=F32
        )
        for b in range(2):
            sbx1[t // 4, :, 2 * (t % 4) + b] = v[:, b * 128:(b + 1) * 128].reshape(R, 4, 128).astype(BF)
        return 0

    lax.fori_loop(0, 8, mid_partial, 0)
    remote(sbx1.at[1 - c], rbx1, HX1, (p1, r), rbx1).start()
    arrived(HX1)
    xsum = reduce_half(sbx1, rbx1, sby1, ry1, sz1, lz1, RS1)
    for b in range(8):
        v = (xsum[b] * live(piv1, 8 * c + b)).astype(BF)
        xsb1[b] = v
        zm[1 + 8 * c + b] = v
    remote(xsb1, zm.at[pl.ds(1 + 8 * c, 8)], ZX1, (p1, r), zm.at[pl.ds(0, 8)]).start()
    arrived(ZX1)
    arrived(ZGM)

    def leaf_pick(j, _):
        gl[j] = zm[lt[s, j] + 1]
        return 0

    lax.fori_loop(0, 240, leaf_pick, 0, unroll=8)
    to_rows(lambda d: gl.at[pl.ds(960 * d // 128, 8)], lg0.at[r], GR0, lg0.at[pl.ds(0, R - 1)])
    lg0[r] = gl[pl.ds(960 * r // 128, 8)]
    to_rows(lambda d: xsb1.at[d // 4], lom.at[r], OM, lom.at[pl.ds(0, R - 1)])
    lom[r] = xsb1[r // 4]
    arrived(OT)
    tmp[0:128] = lot[...].astype(F32).reshape(128, 128).T
    o_top[...] = tmp[pl.ds(pl.multiple_of(16 * (r % 8), 16), 16), :].astype(BF)
    arrived(GR0)
    for b in range(8):
        g0[:, b * 128:(b + 1) * 128] = lg0[:, b].reshape(128, 128)

    def leaf_tile(o):
        t = (z + o) % 8
        cols = pl.ds(pl.multiple_of(t * 256, 256), 256)
        v = jnp.dot(y0[...], qv0[:, cols], preferred_element_type=F32) - jnp.dot(
            g0[...], wp0[:, cols], preferred_element_type=F32
        )
        sbl[pl.ds(4 * t, 4)] = v.T.astype(BF).reshape(4, 64, 128)
        reduce_y(lambda d: sbl.at[d], ryl, RS0, o, lambda k: ryl.at[0, pl.ds(0, k)])

    def leaf_sum(o):
        return reduce_z(sbl, ryl, szl, lzl, RS0, o, lambda k: lzl.at[pl.ds(0, k)])

    for k in range(8):
        leaf_tile(ORDER[k])
        if k >= 3:
            leaf_sum(ORDER[k - 3])
    for k in range(5, 8):
        xl = leaf_sum(ORDER[k])
    arrived(OM)
    tmp[0:128] = lom[...].astype(F32).reshape(128, 128).T
    o_mid[...] = tmp[pl.ds(pl.multiple_of(32 * (r % 4), 32), 32), :].astype(BF)
    arrived(RS0 + 8)
    for o in range(7):
        xl = xl + lzl[o].astype(F32)
    o_leaf[...] = (xl * f0).astype(BF)

    for n in landed:
        sent(n)


SCRATCH = [
    ((1024, 2048), BF), ((640, 2048), BF), ((384, 2048), BF), ((64, 2048), BF), ((32, 2048), BF), ((16, 2048), BF),
    ((64, 128), BF), ((R, 5, 4, 128), BF),
    ((R, 64, 128), BF), ((128, 2048), BF), ((128, 64), BF), ((128, 32), BF), ((128, 16), BF), ((R, 5, 4, 128), BF),
    ((R, 8, 4, 128), BF), ((264, 4, 128), BF), ((128, 4, 128), BF), ((128, 4, 128), BF), ((128, 4, 128), F32),
    ((8, 4, 128), F32), ((8, 4, 128), BF), ((2, R, 8, 4, 128), BF), ((R, 5, 4, 128), BF), ((R, 5, 4, 128), BF),
    ((122, 4, 128), BF),
    ((16, 4, 128), BF), ((3, 16, 4, 128), BF), ((3, 60, 4, 128), BF), ((3, 60, 4, 128), BF), ((16, 4, 128), BF),
    ((16, 4, 128), BF), ((2, R, 8, 4, 128), BF), ((60, 4, 128), BF), ((257, 4, 128), BF), ((61, 4, 128), BF),
    ((R, 3, 4, 128), BF), ((128, 384), BF), ((128, 2048), F32), ((2, R, 8, 4, 128), BF), ((R, 8, 4, 128), BF),
    ((R, 8, 4, 128), BF), ((8, 3, 8, 4, 128), BF), ((7, 8, 4, 128), BF), ((7, 8, 4, 128), BF), ((8, 4, 128), F32), ((8, 4, 128), F32), ((121, 4, 128), BF),
    ((257, 4, 128), BF), ((R, 5, 4, 128), BF), ((128, 640), BF),
    ((2, R, 8, 4, 128), BF), ((R, 8, 4, 128), BF), ((R, 8, 4, 128), BF), ((8, 3, 8, 4, 128), BF), ((7, 8, 4, 128), BF), ((7, 8, 4, 128), BF), ((8, 4, 128), BF),
    ((240, 4, 128), BF), ((R, 8, 4, 128), BF), ((128, 1024), BF), ((R, 64, 128), BF), ((8, 3, 64, 128), BF),
    ((7, 64, 128), BF), ((7, 64, 128), BF),
    ((R, 4, 128), BF), ((R, 4, 128), BF),
]


def hand_over(*refs):
    for k in range(4):
        refs[4 + k][...] = refs[k][...]


def body(
    leaf_inverse, leaf_panel, mid_inverse, mid_panel, top_inverse, top_panel,
    leaf_rhs, mid_rhs, top_rhs, outer_solution, leaf_targets, mid_targets, front_counts,
):
    vmem = pl.BlockSpec(memory_space=pltpu.VMEM)
    smem = pl.BlockSpec(memory_space=pltpu.SMEM)
    hbm = pl.BlockSpec(memory_space=pl.ANY)
    outs = pl.pallas_call(
        kernel,
        out_shape=tuple(jax.ShapeDtypeStruct((n, 128), BF) for n in (64, 32, 16, 240)),
        in_specs=[vmem] * 4 + [hbm] * 6 + [vmem] * 2 + [smem] * 3,
        out_specs=(vmem,) * 4,
        scratch_shapes=[pltpu.VMEM(shape, kind) for shape, kind in SCRATCH]
        + [pltpu.VMEM((384, 128), F32), pltpu.VMEM((8, 128), jnp.int32), pltpu.SMEM((8, 128), jnp.int32)]
        + [pltpu.SemaphoreType.DMA, pltpu.SemaphoreType.DMA((6,)), pltpu.SemaphoreType.DMA((NSEM,)), pltpu.SemaphoreType.DMA((NSEM,))],
        compiler_params=pltpu.CompilerParams(
            collective_id=0, has_side_effects=True, vmem_limit_bytes=56 * 1024 * 1024
        ),
        name="solve",
    )(
        leaf_rhs.T, mid_rhs.T, top_rhs.T, outer_solution.T,
        leaf_panel, leaf_inverse, mid_panel, mid_inverse, top_panel, top_inverse,
        leaf_targets, mid_targets, leaf_targets, mid_targets, front_counts.T,
    )
    shapes = tuple(jax.ShapeDtypeStruct(out.shape, BF) for out in outs)
    outs = pl.pallas_call(hand_over, out_shape=shapes, in_specs=[vmem] * 4, out_specs=(vmem,) * 4, name="hand_over")(*outs)
    return tuple(out.T for out in outs)


def solution(mesh):
    stacked = P(("leaf", "rows"), None)
    side = P(None, ("leaf", "rows"))
    return jax.shard_map(
        body,
        mesh=mesh,
        in_specs=(stacked,) * 6 + (side,) * 4 + (P(),) * 3,
        out_specs=(side,) * 4,
        check_vma=False,
    )
```

time: 1130 us -> 136 us (0.12); the launches traced: 1120 us -> 135 us
  waiting for transfers between devices: 695 us -> 0 us
  local copies, waits for them, and re-layouts: 139 us -> 0 us
  blocking collectives: 139 us -> 0 us
  Pallas kernels: 0 us -> 135 us
  starting transfers between devices: 92.1 us -> 0 us
  matrix products: 22.4 us -> 0 us
  between operations: 14.9 us -> 0.64 us
  other arithmetic: 13.2 us -> 0 us
    reduce_scatter x3 -> x0, waiting for transfers between devices: 622 us -> none  [separate_sums(): lax.psum_scatter(shaped.astype(jnp.bfloat16), 'rows', scatter_dimension=2...]
    pallas_call x0 -> x2, Pallas kernels: none -> 135 us  [the longest x1 133 us: body(): pl.pallas_call(kernel, out_shape=tuple((jax.ShapeDtypeStruct((n, 128), BF...]
    all_gather x3 -> x0, blocking collectives: 108 us -> none  [body(): gathered = lax.all_gather(assembled_local, 'rows', axis=1, tiled=True)]
    unnamed x42 -> x0, local copies, waits for them, and re-layouts: 75.2 us -> none
    ppermute x12 -> x0, starting transfers between devices: 65.7 us -> none  [from_partner(): return lax.ppermute(value, axis, pairs)]
    all_to_all x6 -> x0, waiting for transfers between devices: 55.7 us -> none  [the longest x2 20.8 us: extend_children(): lax.all_to_all(joined.astype(jnp.bfloat16), 'rows', split_axis=2, concat_...]
    all_to_all x12 -> x0, local copies, waits for them, and re-layouts: 32.7 us -> none  [the longest x2 27.3 us: extend_children(): lax.all_to_all(joined.astype(jnp.bfloat16), 'rows', split_axis=2, concat_...]
    all_to_all x2 -> x0, blocking collectives: 31 us -> none  [descend_children(): lax.all_to_all(full_local, 'rows', split_axis=0, concat_axis=1, tiled=True)]
  transfers between devices with their start and end apart: 21 -> 0, of which waited for: 20 -> 0; matrix products, arithmetic and copies ran while one was open for 1% -> 0% of each run, Pallas kernels for 0% -> 0%
where the time goes in v1:
time: 136 us; the launch traced here: 135 us
  Pallas kernels  135 us (99%)
    pallas_call x1, Pallas kernels, body(): pl.pallas_call(kernel, out_shape=tuple((jax.ShapeDtypeStruct((n, 128), BF...  133 us

profile of v1, /device:TPU:1, one launch (start us, length us, event | category | flops | bytes accessed | tf_op | source)
XLA Modules:
  0.0 135.3 jit_solution(9803574040775198713)
XLA Ops:
  0.6 133.2 %solve.1 = (bf16[64,128]{1,0:T(8,128)(2,1)}, bf16[32,128]{1,0:T(8,128)(2,1)}, bf16[16,128]{1,0:T(8,128)(2,1)}, bf16[240,128]{1,0:T(8,128)(2,1)}) custom-call(bf16[64,128]{1,0:T(8,128)(2,1)} %bitcast.10, bf16[32,128]{1,0:T(8,128)(2,1)} %bitcast.11, bf16[16,128]{1,0:T(8,128)(2,1)} %bitcast.12, bf16[240,128]{1,0:T(8,128)(2,1)} %bitcast.9, ...), custom_call_target="tpu_custom_call" | custom-call | tf_op jit(solution)/shard_map/solve/pallas_call | solution.py:490
  133.8 1.5 %hand_over.1 = (bf16[64,128]{1,0:T(8,128)(2,1)}, bf16[32,128]{1,0:T(8,128)(2,1)}, bf16[16,128]{1,0:T(8,128)(2,1)}, bf16[240,128]{1,0:T(8,128)(2,1)}) custom-call(bf16[64,128]{1,0:T(8,128)(2,1)} %get-tuple-element.12.refs_0_, bf16[32,128]{1,0:T(8,128)(2,1)} %get-tuple-element.13.refs_1_, bf16[16,128]{1,0:T(8,128)(2,1)} %get-tuple-element.14.refs_2_, ...), custom_call_target="tpu_custom_call" | custom-call | tf_op jit(solution)/shard_map/hand_over/pallas_call | solution.py:508

commit v2 on v1

--- a/solution.py
+++ b/solution.py
@@ -10,9 +10,10 @@
 F32 = jnp.float32
 R = 32
 
-(EA, A1, X1, D1, A2, RT, ZG, P3, U3, D2, CR, HX2, XX2, ZX2, GR1, ZGM, OT, HX1, ZX1, OM, GR0,
- AG0, G1, G2, RS2, RS1, RS0) = tuple(range(21)) + tuple(range(21, 21 + 54, 9))
-NSEM = 21 + 54
+(EA, A1, X1, D1, A2, RT, ZG, P3, U3, D2, CR, HX2, XX2, ZX2, GR1, ZGM, OT, HX1, ZX1, OM, GR0, ZGL,
+ AG0, G1, G2, RS2, RS1, RS0) = tuple(range(22)) + tuple(range(22, 22 + 54, 9))
+NSEM = 22 + 54
+LATE = 5
 
 
 def pieces(rows, period):
@@ -34,7 +35,7 @@
     rhs0, rhs1, rhs2, outer, w0, q0, w1, q1, w2, q2, ltv, mtv, lt, mt, cnt,
     o_leaf, o_mid, o_top, o_con,
     wp0, wp1, wp2, qv0, qv1, qv2, at0, e, at, a, y0, y1, y2, le, sb1, lb1, sp1, rp1, c1, rm, sba1, la1, sb2, lb2, vm,
-    s3p, r3p, s3u, r3u, rtq, sba2, la2, gtq, zt, ct, lc, g2, xpt, sbx, rbx, sby, ry, sz, lz, xs2, xx2, gm, zm, lg1,
+    s3p, r3p, s3u, r3u, rtq, sba2, la2, gtq, zt, ct, lc, g2, xpt, sbx, rbx, sby, ry, sz, lz, xs2, xx2, gm, gml, zm, lg1,
     g1, sbx1, rbx1, sby1, ry1, sz1, lz1, xsb1, gl, lg0, g0, sbl, ryl, szl, lzl, lot, lom,
     tmp, invv, inv, isem, wsem, ssem, rsem,
 ):
@@ -84,8 +85,8 @@
     vm[0] = zero_block
     vm[121] = zero_block
     ct[60] = zero_block
-    zt[0] = zero_block
-    zm[0] = zero_block
+    zt[0:17] = jnp.zeros((17, 4, 128), BF)
+    zm[0:17] = jnp.zeros((17, 4, 128), BF)
     gm[120] = zero_block
 
     piv0, piv1, piv2, upd2 = cnt[0, s], cnt[0, 8 + s // 2], cnt[0, 12 + s // 4], cnt[1, 12 + s // 4]
@@ -157,6 +158,26 @@
         ref = landed[n][0]
         pltpu.make_async_copy(ref, ref, ssem.at[n]).wait()
 
+    def to_early_rows(src_of, dst, n, land):
+        def send(k, _):
+            d = (r + k) % R
+
+            @pl.when(d >= LATE)
+            def _():
+                remote(src_of(d), dst, n, (s, d), land).start()
+            return 0
+
+        lax.fori_loop(1, R, send, 0)
+
+    def to_late_rows(src_of, dst, n, land):
+        def send(d, _):
+            @pl.when(d != r)
+            def _():
+                remote(src_of(d), dst, n, (s, d), land).start()
+            return 0
+
+        lax.fori_loop(0, LATE, send, 0)
+
     def gather(mine, dst, n, piece):
         def along_y(src, k):
             for j in (1, 3, 2):
@@ -238,6 +259,19 @@
 
     lax.fori_loop(0, 8, top_given, 0)
 
+    arrived(ZG)
+
+    def mid_pick(j, _):
+        v = zt[mt[s // 2, 120 * c + j] + 1]
+        gm[j] = v
+        zm[17 + 120 * c + j] = v
+        return 0
+
+    lax.fori_loop(0, 120, mid_pick, 0, unroll=8)
+    for j in range(16, 20):
+        gml[j] = gm[j]
+    remote(gm.at[pl.ds(0, 120)], zm.at[pl.ds(17 + 120 * c, 120)], ZGM, (p1, r), zm.at[pl.ds(0, 120)]).start()
+
     arrived(A1)
     table.wait()
 
@@ -270,6 +304,8 @@
     la1[c, r] = sba1[...]
     gather(sba1, lambda k: la1.at[c, k], G1, lambda k: la1.at[0, pl.ds(0, k)])
     remote(la1.at[c], la1.at[c], D1, (p1, r), la1.at[1 - c]).start()
+    to_early_rows(lambda d: gm.at[pl.ds(480 * d // 128, 5)], lg1.at[r], GR1, lg1.at[pl.ds(0, R - 1)])
+    lg1[r] = gm[pl.ds(480 * r // 128, 5)]
     arrived(D1)
     for h in range(2):
         for b in range(8):
@@ -286,7 +322,15 @@
     to_rows(lambda d: sb2.at[d], lb2.at[r], A2, lb2.at[pl.ds(0, R - 1)])
     lb2[r] = sb2[r]
     y1[...] = (nt(a[...], qv1[...]) * f1).astype(BF)
+    arrived(ZGM)
+
+    def leaf_pick(j, _):
+        gl[j] = zm[lt[s, j] + 1]
+        return 0
+
+    lax.fori_loop(32, 240, leaf_pick, 0, unroll=8)
     arrived(A2)
+    to_early_rows(lambda d: gl.at[pl.ds(960 * d // 128, 8)], lg0.at[r], GR0, lg0.at[pl.ds(0, R - 1)])
 
     def mid_merge(q, _):
         for i, parts in enumerate(MID_PIECES):
@@ -371,18 +415,18 @@
         zt[1 + 8 * c + b] = ((xs2[b] + xx2[b]) * live(piv2, 8 * c + b)).astype(BF)
     remote(zt.at[pl.ds(1 + 8 * c, 8)], zt.at[pl.ds(1 + 8 * c, 8)], ZX2, (p1, r), zt.at[pl.ds(0, 8)]).start()
     arrived(ZX2)
-    arrived(ZG)
-
-    def mid_pick(j, _):
+
+    for j in range(16):
         v = zt[mt[s // 2, 120 * c + j] + 1]
-        gm[j] = v
+        gml[j] = v
         zm[17 + 120 * c + j] = v
-        return 0
-
-    lax.fori_loop(0, 120, mid_pick, 0, unroll=8)
-    to_rows(lambda d: gm.at[pl.ds(480 * d // 128, 5)], lg1.at[r], GR1, lg1.at[pl.ds(0, R - 1)])
-    lg1[r] = gm[pl.ds(480 * r // 128, 5)]
-    remote(gm.at[pl.ds(0, 120)], zm.at[pl.ds(17 + 120 * c, 120)], ZGM, (p1, r), zm.at[pl.ds(0, 120)]).start()
+    to_late_rows(lambda d: gml.at[pl.ds(480 * d // 128, 5)], lg1.at[r], GR1, lg1.at[pl.ds(0, R - 1)])
+
+    @pl.when(r < LATE)
+    def _():
+        lg1[r] = gml[pl.ds(480 * jnp.minimum(r, LATE - 1) // 128, 5)]
+
+    remote(gml.at[pl.ds(0, 16)], zm.at[pl.ds(17 + 120 * c, 16)], ZGL, (p1, r), zm.at[pl.ds(0, 16)]).start()
     to_rows(lambda d: zt.at[1 + 4 * w4 + d // 8], lot.at[r], OT, lot.at[pl.ds(0, R - 1)])
     lot[r] = zt[1 + 4 * w4 + r // 8]
     arrived(GR1)
@@ -408,14 +452,10 @@
         zm[1 + 8 * c + b] = v
     remote(xsb1, zm.at[pl.ds(1 + 8 * c, 8)], ZX1, (p1, r), zm.at[pl.ds(0, 8)]).start()
     arrived(ZX1)
-    arrived(ZGM)
-
-    def leaf_pick(j, _):
-        gl[j] = zm[lt[s, j] + 1]
-        return 0
-
-    lax.fori_loop(0, 240, leaf_pick, 0, unroll=8)
-    to_rows(lambda d: gl.at[pl.ds(960 * d // 128, 8)], lg0.at[r], GR0, lg0.at[pl.ds(0, R - 1)])
+    arrived(ZGL)
+
+    lax.fori_loop(0, 32, leaf_pick, 0, unroll=8)
+    to_late_rows(lambda d: gl.at[pl.ds(960 * d // 128, 8)], lg0.at[r], GR0, lg0.at[pl.ds(0, R - 1)])
     lg0[r] = gl[pl.ds(960 * r // 128, 8)]
     to_rows(lambda d: xsb1.at[d // 4], lom.at[r], OM, lom.at[pl.ds(0, R - 1)])
     lom[r] = xsb1[r // 4]
@@ -466,7 +506,7 @@
     ((16, 4, 128), BF), ((3, 16, 4, 128), BF), ((3, 60, 4, 128), BF), ((3, 60, 4, 128), BF), ((16, 4, 128), BF),
     ((16, 4, 128), BF), ((2, R, 8, 4, 128), BF), ((60, 4, 128), BF), ((257, 4, 128), BF), ((61, 4, 128), BF),
     ((R, 3, 4, 128), BF), ((128, 384), BF), ((128, 2048), F32), ((2, R, 8, 4, 128), BF), ((R, 8, 4, 128), BF),
-    ((R, 8, 4, 128), BF), ((8, 3, 8, 4, 128), BF), ((7, 8, 4, 128), BF), ((7, 8, 4, 128), BF), ((8, 4, 128), F32), ((8, 4, 128), F32), ((121, 4, 128), BF),
+    ((R, 8, 4, 128), BF), ((8, 3, 8, 4, 128), BF), ((7, 8, 4, 128), BF), ((7, 8, 4, 128), BF), ((8, 4, 128), F32), ((8, 4, 128), F32), ((121, 4, 128), BF), ((20, 4, 128), BF),
     ((257, 4, 128), BF), ((R, 5, 4, 128), BF), ((128, 640), BF),
     ((2, R, 8, 4, 128), BF), ((R, 8, 4, 128), BF), ((R, 8, 4, 128), BF), ((8, 3, 8, 4, 128), BF), ((7, 8, 4, 128), BF), ((7, 8, 4, 128), BF), ((8, 4, 128), BF),
     ((240, 4, 128), BF), ((R, 8, 4, 128), BF), ((128, 1024), BF), ((R, 64, 128), BF), ((8, 3, 64, 128), BF),

time: 136 us -> 131 us (0.963)
  Pallas kernels: 135 us -> 130 us
    pallas_call x1, Pallas kernels: 133 us -> 129 us  [body(): pl.pallas_call(kernel, out_shape=tuple((jax.ShapeDtypeStruct((n, 128), BF...]
where the time goes in v2:
time: 131 us
  Pallas kernels  130 us (99%)
    pallas_call x1, Pallas kernels, body(): pl.pallas_call(kernel, out_shape=tuple((jax.ShapeDtypeStruct((n, 128), BF...  129 us

profile of v2, /device:TPU:1, one launch (start us, length us, event | category | flops | bytes accessed | tf_op | source)
XLA Modules:
  0.0 131.0 jit_solution(2198379100150705000)
XLA Ops:
  0.6 128.9 %solve.1 = (bf16[64,128]{1,0:T(8,128)(2,1)}, bf16[32,128]{1,0:T(8,128)(2,1)}, bf16[16,128]{1,0:T(8,128)(2,1)}, bf16[240,128]{1,0:T(8,128)(2,1)}) custom-call(bf16[64,128]{1,0:T(8,128)(2,1)} %bitcast.10, bf16[32,128]{1,0:T(8,128)(2,1)} %bitcast.11, bf16[16,128]{1,0:T(8,128)(2,1)} %bitcast.12, bf16[240,128]{1,0:T(8,128)(2,1)} %bitcast.9, ...), custom_call_target="tpu_custom_call" | custom-call | tf_op jit(solution)/shard_map/solve/pallas_call | solution.py:530
  129.5 1.5 %hand_over.1 = (bf16[64,128]{1,0:T(8,128)(2,1)}, bf16[32,128]{1,0:T(8,128)(2,1)}, bf16[16,128]{1,0:T(8,128)(2,1)}, bf16[240,128]{1,0:T(8,128)(2,1)}) custom-call(bf16[64,128]{1,0:T(8,128)(2,1)} %get-tuple-element.12.refs_0_, bf16[32,128]{1,0:T(8,128)(2,1)} %get-tuple-element.13.refs_1_, bf16[16,128]{1,0:T(8,128)(2,1)} %get-tuple-element.14.refs_2_, ...), custom_call_target="tpu_custom_call" | custom-call | tf_op jit(solution)/shard_map/hand_over/pallas_call | solution.py:548

commit v3 on v2

--- a/solution.py
+++ b/solution.py
@@ -55,11 +55,10 @@
 
     barrier = pltpu.get_barrier_semaphore()
 
-    def greet(k, _):
-        pl.semaphore_signal(barrier, inc=1, device_id=(s, (r + k) % R), device_id_type=MESH)
-        return 0
-
-    lax.fori_loop(1, R, greet, 0)
+    for k in range(1, 8):
+        pl.semaphore_signal(barrier, inc=1, device_id=(s, (z + k) % 8 * 4 + y), device_id_type=MESH)
+    for k in range(1, 4):
+        pl.semaphore_signal(barrier, inc=1, device_id=(s, z * 4 + (y + k) % 4), device_id_type=MESH)
     for p in partners:
         pl.semaphore_signal(barrier, inc=1, device_id=(p, r), device_id_type=MESH)
 
@@ -131,7 +130,7 @@
         g2[:, b * 128:(b + 1) * 128] = v.astype(BF)
         e[:, 2 + b] = v.reshape(R, 4, 128).astype(BF)
 
-    pl.semaphore_wait(barrier, R - 1 + 3)
+    pl.semaphore_wait(barrier, 7 + 3 + 3)
 
     landed = {}
 
@@ -206,7 +205,7 @@
         stage[o - 1] = v.astype(BF)
         remote(stage.at[o - 1], final.at[o - 1], n + 8, (s, t * 4 + y), piece(7)).start()
 
-    ORDER = (1, 2, 3, 4, 5, 6, 7, 0)
+    ORDER = (4, 3, 5, 2, 6, 1, 7, 0)
 
     def nt(x, w):
         return lax.dot_general(x, w, (((1,), (1,)), ((), ())), preferred_element_type=F32)
@@ -313,12 +312,10 @@
     loads[2].wait()
     loads[3].wait()
 
-    def mid_update(t, _):
-        prod = nt(a[...], wp1[pl.ds(pl.multiple_of(t * 128, 128), 128), :])
-        sb2[:, t] = prod.reshape(R, 4, 128).astype(BF)
-        return 0
-
-    lax.fori_loop(0, 5, mid_update, 0)
+    for t in range(0, 5, 2):
+        prod = nt(a[...], wp1[t * 128:min(t + 2, 5) * 128, :])
+        for b in range(t, min(t + 2, 5)):
+            sb2[:, b] = prod[:, (b - t) * 128:(b - t + 1) * 128].reshape(R, 4, 128).astype(BF)
     to_rows(lambda d: sb2.at[d], lb2.at[r], A2, lb2.at[pl.ds(0, R - 1)])
     lb2[r] = sb2[r]
     y1[...] = (nt(a[...], qv1[...]) * f1).astype(BF)
@@ -480,9 +477,9 @@
 
     for k in range(8):
         leaf_tile(ORDER[k])
-        if k >= 3:
-            leaf_sum(ORDER[k - 3])
-    for k in range(5, 8):
+        if k >= 4:
+            leaf_sum(ORDER[k - 4])
+    for k in range(4, 8):
         xl = leaf_sum(ORDER[k])
     arrived(OM)
     tmp[0:128] = lom[...].astype(F32).reshape(128, 128).T

time: 131 us -> 129 us (0.985)
    pallas_call x1, Pallas kernels: 129 us -> 127 us  [body(): pl.pallas_call(kernel, out_shape=tuple((jax.ShapeDtypeStruct((n, 128), BF...]
where the time goes in v3:
time: 129 us
  Pallas kernels  129 us (100%)
    pallas_call x1, Pallas kernels, body(): pl.pallas_call(kernel, out_shape=tuple((jax.ShapeDtypeStruct((n, 128), BF...  127 us

profile of v3, /device:TPU:1, one launch (start us, length us, event | category | flops | bytes accessed | tf_op | source)
XLA Modules:
  0.0 129.3 jit_solution(8767788541011262858)
XLA Ops:
  0.6 127.1 %solve.1 = (bf16[64,128]{1,0:T(8,128)(2,1)}, bf16[32,128]{1,0:T(8,128)(2,1)}, bf16[16,128]{1,0:T(8,128)(2,1)}, bf16[240,128]{1,0:T(8,128)(2,1)}) custom-call(bf16[64,128]{1,0:T(8,128)(2,1)} %bitcast.10, bf16[32,128]{1,0:T(8,128)(2,1)} %bitcast.11, bf16[16,128]{1,0:T(8,128)(2,1)} %bitcast.12, bf16[240,128]{1,0:T(8,128)(2,1)} %bitcast.9, ...), custom_call_target="tpu_custom_call" | custom-call | tf_op jit(solution)/shard_map/solve/pallas_call | solution.py:527
  127.8 1.5 %hand_over.1 = (bf16[64,128]{1,0:T(8,128)(2,1)}, bf16[32,128]{1,0:T(8,128)(2,1)}, bf16[16,128]{1,0:T(8,128)(2,1)}, bf16[240,128]{1,0:T(8,128)(2,1)}) custom-call(bf16[64,128]{1,0:T(8,128)(2,1)} %get-tuple-element.12.refs_0_, bf16[32,128]{1,0:T(8,128)(2,1)} %get-tuple-element.13.refs_1_, bf16[16,128]{1,0:T(8,128)(2,1)} %get-tuple-element.14.refs_2_, ...), custom_call_target="tpu_custom_call" | custom-call | tf_op jit(solution)/shard_map/hand_over/pallas_call | solution.py:545

commit v4 on v3

--- a/solution.py
+++ b/solution.py
@@ -207,6 +207,11 @@
 
     ORDER = (4, 3, 5, 2, 6, 1, 7, 0)
 
+    def spread_half(landing, h):
+        for b in range(8):
+            cols = pl.ds(pl.multiple_of((8 * h + b) * 128, 128), 128)
+            a[:, cols] = landing[h, :, b].reshape(128, 128)
+
     def nt(x, w):
         return lax.dot_general(x, w, (((1,), (1,)), ((), ())), preferred_element_type=F32)
 
@@ -305,10 +310,9 @@
     remote(la1.at[c], la1.at[c], D1, (p1, r), la1.at[1 - c]).start()
     to_early_rows(lambda d: gm.at[pl.ds(480 * d // 128, 5)], lg1.at[r], GR1, lg1.at[pl.ds(0, R - 1)])
     lg1[r] = gm[pl.ds(480 * r // 128, 5)]
+    spread_half(la1, c)
     arrived(D1)
-    for h in range(2):
-        for b in range(8):
-            a[:, (8 * h + b) * 128:(8 * h + b + 1) * 128] = la1[h, :, b].reshape(128, 128)
+    spread_half(la1, 1 - c)
     loads[2].wait()
     loads[3].wait()
 
@@ -369,10 +373,9 @@
     remote(la2.at[c], la2.at[c], D2, (p1, r), la2.at[1 - c]).start()
     to_rows(lambda d: ct.at[pl.ds(240 * d // 128, 3)], lc.at[r], CR, lc.at[pl.ds(0, R - 1)])
     lc[r] = ct[pl.ds(240 * r // 128, 3)]
+    spread_half(la2, c)
     arrived(D2)
-    for h in range(2):
-        for b in range(8):
-            a[:, (8 * h + b) * 128:(8 * h + b + 1) * 128] = la2[h, :, b].reshape(128, 128)
+    spread_half(la2, 1 - c)
     y2[...] = (nt(a[...], qv2[...]) * f2).astype(BF)
 
     def top_partial(t, _):
@@ -430,7 +433,8 @@
     for b in range(5):
         g1[:, b * 128:(b + 1) * 128] = lg1[:, b].reshape(128, 128)
 
-    def mid_partial(t, _):
+    def mid_partial(i, _):
+        t = (4 * (1 - c) + i) % 8
         cols = pl.ds(pl.multiple_of(t * 256, 256), 256)
         v = jnp.dot(y1[...], qv1[:, cols], preferred_element_type=F32) - jnp.dot(
             g1[...], wp1[:, cols], preferred_element_type=F32
@@ -439,8 +443,9 @@
             sbx1[t // 4, :, 2 * (t % 4) + b] = v[:, b * 128:(b + 1) * 128].reshape(R, 4, 128).astype(BF)
         return 0
 
-    lax.fori_loop(0, 8, mid_partial, 0)
+    lax.fori_loop(0, 4, mid_partial, 0)
     remote(sbx1.at[1 - c], rbx1, HX1, (p1, r), rbx1).start()
+    lax.fori_loop(4, 8, mid_partial, 0)
     arrived(HX1)
     xsum = reduce_half(sbx1, rbx1, sby1, ry1, sz1, lz1, RS1)
     for b in range(8):

time: 129 us -> 129 us (level)
  no operation moved by 1% of the time
where the time goes in v4:
time: 129 us; the launch traced here: 128 us
  Pallas kernels  128 us (99%)
    pallas_call x1, Pallas kernels, body(): pl.pallas_call(kernel, out_shape=tuple((jax.ShapeDtypeStruct((n, 128), BF...  126 us

profile of v4, /device:TPU:1, one launch (start us, length us, event | category | flops | bytes accessed | tf_op | source)
XLA Modules:
  0.0 128.4 jit_solution(10633806837332538202)
XLA Ops:
  0.6 126.3 %solve.1 = (bf16[64,128]{1,0:T(8,128)(2,1)}, bf16[32,128]{1,0:T(8,128)(2,1)}, bf16[16,128]{1,0:T(8,128)(2,1)}, bf16[240,128]{1,0:T(8,128)(2,1)}) custom-call(bf16[64,128]{1,0:T(8,128)(2,1)} %bitcast.10, bf16[32,128]{1,0:T(8,128)(2,1)} %bitcast.11, bf16[16,128]{1,0:T(8,128)(2,1)} %bitcast.12, bf16[240,128]{1,0:T(8,128)(2,1)} %bitcast.9, ...), custom_call_target="tpu_custom_call" | custom-call | tf_op jit(solution)/shard_map/solve/pallas_call | solution.py:532
  126.9 1.5 %hand_over.1 = (bf16[64,128]{1,0:T(8,128)(2,1)}, bf16[32,128]{1,0:T(8,128)(2,1)}, bf16[16,128]{1,0:T(8,128)(2,1)}, bf16[240,128]{1,0:T(8,128)(2,1)}) custom-call(bf16[64,128]{1,0:T(8,128)(2,1)} %get-tuple-element.12.refs_0_, bf16[32,128]{1,0:T(8,128)(2,1)} %get-tuple-element.13.refs_1_, bf16[16,128]{1,0:T(8,128)(2,1)} %get-tuple-element.14.refs_2_, ...), custom_call_target="tpu_custom_call" | custom-call | tf_op jit(solution)/shard_map/hand_over/pallas_call | solution.py:550
